TPU v7x, 32 devices: a whole 2x2x4 slice. The times are simulated.
32 devices in a mesh: seq: 16 (over z, y, x), head: 2 (over core).
Axes of the slice: x: 2, y: 2, z: 4, core: 2. Of those that a mesh axis runs over, the one named last changes fastest.
Arguments:
- block_in: bfloat16 [3072, 1024], P('seq'), may hold values from -6 to 6
- first_norm_gain: float32 [1024], replicated, may hold values from 0.25 to 1.75
- w_query: bfloat16 [1024, 1024], P('seq', 'head'), may hold values from -0.1875 to 0.1875
- w_key: bfloat16 [1024, 1024], P('seq', 'head'), may hold values from -0.1875 to 0.1875
- w_value: bfloat16 [1024, 2048], P('seq', 'head'), may hold values from -0.1875 to 0.1875
- w_gate: bfloat16 [1024, 2048], P('seq', 'head'), may hold values from -0.1875 to 0.1875
- w_alpha: bfloat16 [1024, 8], P('seq', 'head'), may hold values from -0.1875 to 0.1875
- w_beta: bfloat16 [1024, 8], P('seq', 'head'), may hold values from -0.1875 to 0.1875
- conv_query: float32 [4, 1024], P(None, 'head'), may hold values from -3 to 3
- conv_key: float32 [4, 1024], P(None, 'head'), may hold values from -3 to 3
- conv_value: float32 [4, 2048], P(None, 'head'), may hold values from -3 to 3
- a_log: float32 [8], P('head'), may hold values from -9 to 1
- dt_bias: float32 [8], P('head'), may hold values from -4 to 1
- out_gain: float32 [256], replicated, may hold values from 0.25 to 1.75
- w_out: bfloat16 [2048, 1024], P('head', 'seq'), may hold values from -0.1875 to 0.1875
- second_norm_gain: float32 [1024], replicated, may hold values from 0.25 to 1.75
- w_ffgate: bfloat16 [1024, 2816], P('seq', 'head'), may hold values from -0.1875 to 0.1875
- w_ffup: bfloat16 [1024, 2816], P('seq', 'head'), may hold values from -0.1875 to 0.1875
- w_ffdown: bfloat16 [2816, 1024], P('head', 'seq'), may hold values from -0.21875 to 0.21875
- cotangent: bfloat16 [3072, 1024], P('seq'), may hold values from -6 to 6
Outputs:
- block_out: bfloat16 [3072, 1024], P('seq')
- input_gradient: float32 [3072, 1024], P('seq')
- first_norm_gain_gradient: float32 [1024], replicated
- grad_query: float32 [1024, 1024], P('seq', 'head')
- grad_key: float32 [1024, 1024], P('seq', 'head')
- grad_value: float32 [1024, 2048], P('seq', 'head')
- grad_gate: float32 [1024, 2048], P('seq', 'head')
- grad_alpha: float32 [1024, 8], P('seq', 'head')
- grad_beta: float32 [1024, 8], P('seq', 'head')
- grad_convq: float32 [4, 1024], P(None, 'head')
- grad_convk: float32 [4, 1024], P(None, 'head')
- grad_convv: float32 [4, 2048], P(None, 'head')
- grad_alog: float32 [8], P('head')
- grad_dt: float32 [8], P('head')
- grad_outgain: float32 [256], replicated
- grad_out: float32 [2048, 1024], P('head', 'seq')
- second_norm_gain_gradient: float32 [1024], replicated
- grad_ffgate: float32 [1024, 2816], P('seq', 'head')
- grad_ffup: float32 [1024, 2816], P('seq', 'head')
- grad_ffdown: float32 [2816, 1024], P('head', 'seq')
All inputs are finite; a program needn't handle non-finite values.
Results may differ from a plain program's by a relative error of at most 0.02.
The roundings to bfloat16 on the way count: a program that leaves them out, or rounds other values in their place, can miss the bound.
Values may be sent and summed in bfloat16 or wider, within the bound.
A program may use at most 384 MiB of HBM per device.

v0:
```python
import jax
import jax.numpy as jnp
from jax import lax
from jax.sharding import PartitionSpec as P

CONV = 4
SPAN = 64


MATMUL_ACCURACY = lax.Precision.HIGHEST
EPS_NORM = 1e-06
EPS_HEAD = 1e-05
EPS_UNIT = 1e-06


def from_behind(block, axis, distance):
    devices = range(lax.axis_size(axis))
    route = [(i - distance, i) for i in devices if i - distance in devices]
    return lax.ppermute(block, axis, route)


def prefix(array, axis, join, neutral):
    place = lax.axis_index(axis)
    gathered = jax.tree.map(
        lambda a, kind: lax.all_gather(a.astype(kind), axis), array, (jnp.bfloat16, jnp.bfloat16)
    )
    state = jax.tree.map(lambda a, e: jnp.zeros_like(a) + jnp.asarray(e, a.dtype), array, neutral)

    def one(turn, state):
        return join(
            state,
            jax.tree.map(
                lambda a, own: lax.dynamic_index_in_dim(a, turn, 0, False).astype(own.dtype),
                gathered,
                array,
            ),
        )

    return lax.fori_loop(0, place, one, state)


def entering(array, axis, combine, identity):
    size, mine = (lax.axis_size(axis), lax.axis_index(axis))
    everything = jax.tree.map(
        lambda part, kind: lax.all_gather(part.astype(kind), axis),
        array,
        jax.tree.map(lambda a: jnp.bfloat16 if a.dtype == jnp.float32 else a.dtype, array),
    )
    start = jax.tree.map(
        lambda part, zero: jnp.broadcast_to(jnp.asarray(zero, part.dtype), part.shape),
        array,
        identity,
    )

    def turn(k, before):
        at = size - 1 - k
        reached = at > mine
        new = combine(
            before, jax.tree.map(lambda part, own: part[at].astype(own.dtype), everything, array)
        )
        return jax.tree.map(lambda a, b: jnp.where(reached, a, b), new, before)

    return lax.fori_loop(0, size, turn, start)


def matmul(left, right):
    return jnp.dot(left, right, preferred_element_type=jnp.float32)


def matmul_tl(left, right):
    return lax.dot_general(
        left, right, (((0,), (0,)), ((), ())), preferred_element_type=jnp.float32
    )


def matmul_tr(left, right):
    return lax.dot_general(
        left, right, (((1,), (1,)), ((), ())), preferred_element_type=jnp.float32
    )


def rms_scale(values):
    return lax.rsqrt(jnp.mean(values * values, axis=-1, keepdims=True) + EPS_NORM)


def norm_gradient_step(unit_input_gradient, unit_input, inverse_scale):
    return inverse_scale * (
        unit_input_gradient
        - unit_input * jnp.mean(unit_input_gradient * unit_input, axis=-1, keepdims=True)
    )


def conv_apply(extended, weight, rows):
    total = weight[0] * extended[0:rows]
    for tap in range(1, CONV):
        total = total + weight[tap] * extended[tap : tap + rows]
    return total


def conv_back_apply(extended, weight, rows):
    total = weight[0] * extended[CONV - 1 : CONV - 1 + rows]
    for tap in range(1, CONV):
        total = total + weight[tap] * extended[CONV - 1 - tap : CONV - 1 - tap + rows]
    return total


def conv_weight_grad(grad_out, extended, rows):
    return jnp.stack(
        [jnp.sum(grad_out * extended[tap : tap + rows], axis=0) for tap in range(CONV)], axis=0
    )


def prepare(qc, kc, vc, b_lin, a_lin, a_log, dt_bias):
    heads = a_log.shape[0]
    rows = qc.shape[0]
    q_act = jax.nn.silu(qc).reshape(rows, heads, -1)
    k_act = jax.nn.silu(kc).reshape(rows, heads, -1)
    dim_k = q_act.shape[-1]
    query = (
        q_act
        * lax.rsqrt(jnp.sum(q_act * q_act, axis=-1, keepdims=True) + EPS_UNIT)
        * dim_k ** (-0.5)
    )
    keyvec = k_act * lax.rsqrt(jnp.sum(k_act * k_act, axis=-1, keepdims=True) + EPS_UNIT)
    value = jax.nn.silu(vc).reshape(rows, heads, -1)
    beta = jax.nn.sigmoid(b_lin).T
    logdec = (-jnp.exp(a_log)[None, :] * jax.nn.softplus(a_lin + dt_bias[None, :])).T
    return (
        jnp.transpose(query, (1, 0, 2)),
        jnp.transpose(keyvec, (1, 0, 2)),
        jnp.transpose(value, (1, 0, 2)),
        beta,
        logdec,
    )


def span_terms(query, keyvec, value, beta, logdec):
    size = query.shape[1]
    dim_k = keyvec.shape[-1]
    dim_v = value.shape[-1]
    cumul = jnp.cumsum(logdec, axis=-1)
    index = jnp.arange(size)
    strict = index[:, None] > index[None, :]
    weak = index[:, None] >= index[None, :]
    diff = cumul[:, :, None] - cumul[:, None, :]
    decay = jnp.where(weak, jnp.exp(jnp.where(weak, diff, 0.0)), 0.0)
    kk = jnp.einsum("hck,hdk->hcd", keyvec, keyvec, precision=MATMUL_ACCURACY)
    lower = jnp.where(strict, beta[:, :, None] * decay * kk, 0.0) + jnp.eye(size, dtype=query.dtype)
    rhs = jnp.concatenate(
        [beta[:, :, None] * value, (beta * jnp.exp(cumul))[:, :, None] * keyvec], axis=-1
    )
    solved = lax.linalg.triangular_solve(lower, rhs, left_side=True, lower=True, unit_diagonal=True)
    starting_value = solved[..., :dim_v]
    mixk = solved[..., dim_v:]
    scores = jnp.einsum("hck,hdk->hcd", query, keyvec, precision=MATMUL_ACCURACY) * decay
    empty_output = jnp.einsum("hcd,hdv->hcv", scores, starting_value, precision=MATMUL_ACCURACY)
    extent = jnp.exp(cumul)[:, :, None] * query - jnp.einsum(
        "hcd,hdk->hck", scores, mixk, precision=MATMUL_ACCURACY
    )
    trailing_rows = jnp.exp(cumul[:, -1:] - cumul)[:, :, None] * keyvec
    state_matrix = jnp.exp(cumul[:, -1])[:, None, None] * jnp.eye(
        dim_k, dtype=query.dtype
    ) - jnp.einsum("hck,hcj->hkj", trailing_rows, mixk, precision=MATMUL_ACCURACY)
    addend_update = jnp.einsum(
        "udw,udf->uwf", trailing_rows, starting_value, precision=MATMUL_ACCURACY
    )
    return (empty_output, extent, state_matrix, addend_update)


def local_mix(query, keyvec, value, beta, logdec):
    heads, rows, dim_k = query.shape
    dim_v = value.shape[-1]
    blocks = rows // SPAN

    def split(array):
        return jnp.moveaxis(array.reshape((heads, blocks, SPAN) + array.shape[2:]), 1, 0)

    def step(carry, item):
        product, running_total = carry
        empty_output, extent, state_matrix, addend_update = span_terms(*item)
        empty_output = empty_output + jnp.einsum(
            "aow,awr->aor", extent, running_total, precision=MATMUL_ACCURACY
        )
        extent = jnp.einsum("hck,hkj->hcj", extent, product, precision=MATMUL_ACCURACY)
        product = jnp.einsum("hkj,hji->hki", state_matrix, product, precision=MATMUL_ACCURACY)
        running_total = (
            jnp.einsum("sug,sgc->suc", state_matrix, running_total, precision=MATMUL_ACCURACY)
            + addend_update
        )
        return ((product, running_total), (empty_output, extent))

    eye_stack = jnp.broadcast_to(jnp.eye(dim_k, dtype=query.dtype), (heads, dim_k, dim_k))
    init = (eye_stack, jnp.zeros((heads, dim_k, dim_v), query.dtype))
    (product, running_total), (outputs, reaches) = lax.scan(
        step, init, (split(query), split(keyvec), split(value), split(beta), split(logdec))
    )

    def merge_rows(array):
        return jnp.moveaxis(array, 0, 1).reshape(heads, rows, array.shape[-1])

    return (merge_rows(outputs), merge_rows(reaches), product, running_total)


def finish(block_result, gate_pre, out_gain):
    heads, rows, dim_v = block_result.shape
    normed = (
        block_result
        * lax.rsqrt(jnp.mean(block_result * block_result, axis=-1, keepdims=True) + EPS_HEAD)
        * out_gain
    )
    gating = jax.nn.silu(gate_pre).reshape(rows, heads, dim_v)
    return (jnp.transpose(normed, (1, 0, 2)) * gating).reshape(rows, heads * dim_v)


def compose(earlier, later):
    return (
        jnp.einsum("hij,hjk->hik", later[0], earlier[0], precision=MATMUL_ACCURACY),
        jnp.einsum("hij,hjk->hik", later[0], earlier[1], precision=MATMUL_ACCURACY) + later[1],
    )


def shards(
    block_in,
    first_norm_gain,
    w_query,
    w_key,
    w_value,
    w_gate,
    w_alpha,
    w_beta,
    conv_query,
    conv_key,
    conv_value,
    a_log,
    dt_bias,
    out_gain,
    w_out,
    second_norm_gain,
    w_ffgate,
    w_ffup,
    w_ffdown,
    cotangent,
):
    rows = block_in.shape[0]
    edge = CONV - 1
    fwd = (
        lax.all_gather(w_query, "seq", axis=0, tiled=True),
        lax.all_gather(w_key, "seq", axis=0, tiled=True),
        lax.all_gather(w_value, "seq", axis=0, tiled=True),
        lax.all_gather(w_gate, "seq", axis=0, tiled=True),
        lax.all_gather(w_alpha, "seq", axis=0, tiled=True),
        lax.all_gather(w_beta, "seq", axis=0, tiled=True),
        lax.all_gather(w_ffgate, "seq", axis=0, tiled=True),
        lax.all_gather(w_ffup, "seq", axis=0, tiled=True),
        lax.all_gather(w_out, "seq", axis=1, tiled=True),
        lax.all_gather(w_ffdown, "seq", axis=1, tiled=True),
    )
    full_q, full_k, full_v, full_g, full_a, full_b, full_fg, full_fu, full_o, full_fd = fwd
    input_float = block_in.astype(jnp.float32)
    first_inverse_scale = rms_scale(input_float)
    first_unit_input = input_float * first_inverse_scale
    first_normed_input = (first_unit_input * first_norm_gain).astype(jnp.bfloat16)
    qpre = matmul(first_normed_input, full_q).astype(jnp.bfloat16)
    kpre = matmul(first_normed_input, full_k).astype(jnp.bfloat16)
    vpre = matmul(first_normed_input, full_v).astype(jnp.bfloat16)
    gpre = matmul(first_normed_input, full_g).astype(jnp.bfloat16)
    a_lin = matmul(first_normed_input, full_a)
    b_lin = matmul(first_normed_input, full_b)
    edges = from_behind((qpre[rows - edge :], kpre[rows - edge :], vpre[rows - edge :]), "seq", 1)
    q_ext = jnp.concatenate([edges[0], qpre], axis=0).astype(jnp.float32)
    k_ext = jnp.concatenate([edges[1], kpre], axis=0).astype(jnp.float32)
    v_ext = jnp.concatenate([edges[2], vpre], axis=0).astype(jnp.float32)
    qc = conv_apply(q_ext, conv_query, rows)
    kc = conv_apply(k_ext, conv_key, rows)
    vc = conv_apply(v_ext, conv_value, rows)
    prepared, prepare_back = jax.vjp(prepare, qc, kc, vc, b_lin, a_lin, a_log, dt_bias)
    (empty_output, extent, product, running_total), local_back = jax.vjp(local_mix, *prepared)
    heads, dim_k, dim_v = running_total.shape
    eye_stack = jnp.broadcast_to(jnp.eye(dim_k, dtype=jnp.float32), (heads, dim_k, dim_k))
    zero_state = jnp.zeros((heads, dim_k, dim_v), jnp.float32)
    _, incoming_state = prefix((product, running_total), "seq", compose, (eye_stack, zero_state))
    block_result = empty_output + jnp.einsum(
        "mry,myc->mrc", extent, incoming_state, precision=MATMUL_ACCURACY
    )
    on_f, finish_back = jax.vjp(finish, block_result, gpre.astype(jnp.float32), out_gain)
    on_b = on_f.astype(jnp.bfloat16)
    mixed = lax.psum(matmul(on_b, full_o).astype(jnp.bfloat16), "head").astype(jnp.float32)
    hidden_residual = input_float + mixed
    second_inverse_scale = rms_scale(hidden_residual)
    second_unit_input = hidden_residual * second_inverse_scale
    second_normed_input = (second_unit_input * second_norm_gain).astype(jnp.bfloat16)
    fg = matmul(second_normed_input, full_fg)
    fu = matmul(second_normed_input, full_fu)
    hid = (jax.nn.silu(fg) * fu).astype(jnp.bfloat16)
    fed = lax.psum(matmul(hid, full_fd).astype(jnp.bfloat16), "head").astype(jnp.float32)
    block_out = (hidden_residual + fed).astype(jnp.bfloat16)
    feedforward_output_gradient = cotangent.astype(jnp.float32)
    grad_ffdown = matmul_tl(hid, cotangent)
    dhid = matmul_tr(cotangent, full_fd)
    sig = jax.nn.sigmoid(fg)
    dfu = (dhid * fg * sig).astype(jnp.bfloat16)
    dfg = (dhid * fu * sig * (1.0 + fg * (1.0 - sig))).astype(jnp.bfloat16)
    grad_ffgate = matmul_tl(second_normed_input, dfg)
    grad_ffup = matmul_tl(second_normed_input, dfu)
    second_normed_gradient_piece = matmul_tr(dfg, full_fg) + matmul_tr(dfu, full_fu)
    second_norm_piece = jnp.sum(second_normed_gradient_piece * second_unit_input, axis=0)
    second_normed_gradient = lax.psum(
        second_normed_gradient_piece.astype(jnp.bfloat16), "head"
    ).astype(jnp.float32)
    hidden_gradient = feedforward_output_gradient + norm_gradient_step(
        second_normed_gradient * second_norm_gain, second_unit_input, second_inverse_scale
    )
    dh_b = hidden_gradient.astype(jnp.bfloat16)
    grad_out = matmul_tl(on_b, dh_b)
    don = matmul_tr(dh_b, full_o)
    output_gradient, dgpre, outgain_part = finish_back(don)
    partial_gradient = jnp.einsum(
        "urd,urg->udg", extent, output_gradient, precision=MATMUL_ACCURACY
    )
    _, final_state_gradient = entering(
        (jnp.transpose(product, (0, 2, 1)), partial_gradient),
        "seq",
        compose,
        (eye_stack, zero_state),
    )
    extent_gradient = jnp.einsum(
        "sqw,saw->sqa", output_gradient, incoming_state, precision=MATMUL_ACCURACY
    )
    product_gradient = jnp.einsum(
        "plt,prt->plr", final_state_gradient, incoming_state, precision=MATMUL_ACCURACY
    )
    grads_prepared = local_back(
        (output_gradient, extent_gradient, product_gradient, final_state_gradient)
    )
    dqc, dkc, dvc, db_lin, da_lin, alog_part, dt_part = prepare_back(grads_prepared)
    nexts = from_behind((dqc[:edge], dkc[:edge], dvc[:edge]), "seq", -1)
    convq_part = conv_weight_grad(dqc, q_ext, rows)
    convk_part = conv_weight_grad(dkc, k_ext, rows)
    convv_part = conv_weight_grad(dvc, v_ext, rows)
    dqb = conv_back_apply(jnp.concatenate([dqc, nexts[0]], axis=0), conv_query, rows).astype(
        jnp.bfloat16
    )
    dkb = conv_back_apply(jnp.concatenate([dkc, nexts[1]], axis=0), conv_key, rows).astype(
        jnp.bfloat16
    )
    dvb = conv_back_apply(jnp.concatenate([dvc, nexts[2]], axis=0), conv_value, rows).astype(
        jnp.bfloat16
    )
    dgb = dgpre.astype(jnp.bfloat16)
    dab = da_lin.astype(jnp.bfloat16)
    dbb = db_lin.astype(jnp.bfloat16)
    grad_query = matmul_tl(first_normed_input, dqb)
    grad_key = matmul_tl(first_normed_input, dkb)
    grad_value = matmul_tl(first_normed_input, dvb)
    grad_gate = matmul_tl(first_normed_input, dgb)
    grad_alpha = matmul_tl(first_normed_input, dab)
    grad_beta = matmul_tl(first_normed_input, dbb)
    first_normed_gradient_piece = (
        matmul_tr(dqb, full_q)
        + matmul_tr(dkb, full_k)
        + matmul_tr(dvb, full_v)
        + matmul_tr(dgb, full_g)
        + matmul_tr(dab, full_a)
        + matmul_tr(dbb, full_b)
    )
    first_norm_piece = jnp.sum(first_normed_gradient_piece * first_unit_input, axis=0)
    first_normed_gradient = lax.psum(
        first_normed_gradient_piece.astype(jnp.bfloat16), "head"
    ).astype(jnp.float32)
    input_gradient = hidden_gradient + norm_gradient_step(
        first_normed_gradient * first_norm_gain, first_unit_input, first_inverse_scale
    )
    grad_alog, grad_dt, grad_convq, grad_convk, grad_convv = lax.psum(
        (alog_part, dt_part, convq_part, convk_part, convv_part), "seq"
    )
    first_norm_gain_gradient, second_norm_gain_gradient, grad_outgain = lax.psum(
        (first_norm_piece, second_norm_piece, outgain_part), ("seq", "head")
    )
    summed = (
        lax.psum_scatter(grad_query, "seq", scatter_dimension=0, tiled=True),
        lax.psum_scatter(grad_key, "seq", scatter_dimension=0, tiled=True),
        lax.psum_scatter(grad_value, "seq", scatter_dimension=0, tiled=True),
        lax.psum_scatter(grad_gate, "seq", scatter_dimension=0, tiled=True),
        lax.psum_scatter(grad_alpha, "seq", scatter_dimension=0, tiled=True),
        lax.psum_scatter(grad_beta, "seq", scatter_dimension=0, tiled=True),
        lax.psum_scatter(grad_out, "seq", scatter_dimension=1, tiled=True),
        lax.psum_scatter(grad_ffgate, "seq", scatter_dimension=0, tiled=True),
        lax.psum_scatter(grad_ffup, "seq", scatter_dimension=0, tiled=True),
        lax.psum_scatter(grad_ffdown, "seq", scatter_dimension=1, tiled=True),
    )
    (
        sum_query,
        sum_key,
        sum_value,
        sum_gate,
        sum_alpha,
        sum_beta,
        sum_out,
        sum_ffgate,
        sum_ffup,
        sum_ffdown,
    ) = summed
    return (
        block_out,
        input_gradient,
        first_norm_gain_gradient,
        sum_query,
        sum_key,
        sum_value,
        sum_gate,
        sum_alpha,
        sum_beta,
        grad_convq,
        grad_convk,
        grad_convv,
        grad_alog,
        grad_dt,
        grad_outgain,
        sum_out,
        second_norm_gain_gradient,
        sum_ffgate,
        sum_ffup,
        sum_ffdown,
    )


def solution(mesh):
    placed = (
        P("seq", None),
        P(),
        P("seq", "head"),
        P("seq", "head"),
        P("seq", "head"),
        P("seq", "head"),
        P("seq", "head"),
        P("seq", "head"),
        P(None, "head"),
        P(None, "head"),
        P(None, "head"),
        P("head"),
        P("head"),
        P(),
        P("head", "seq"),
        P(),
        P("seq", "head"),
        P("seq", "head"),
        P("head", "seq"),
        P("seq", None),
    )
    return jax.shard_map(
        shards,
        mesh=mesh,
        in_specs=placed,
        out_specs=(
            P("seq", None),
            P("seq", None),
            P(),
            P("seq", "head"),
            P("seq", "head"),
            P("seq", "head"),
            P("seq", "head"),
            P("seq", "head"),
            P("seq", "head"),
            P(None, "head"),
            P(None, "head"),
            P(None, "head"),
            P("head"),
            P("head"),
            P(),
            P("head", "seq"),
            P(),
            P("seq", "head"),
            P("seq", "head"),
            P("head", "seq"),
        ),
        check_vma=False,
    )
```

profile of v0, /device:TPU:0, one launch (start us, length us, event | category | flops | bytes accessed | tf_op | source)
XLA Modules:
  0.0 2158.5 jit_solution(13916427652461230231)
XLA Ops:
  12.2 42.8 %all-gather.4 = bf16[16,64,4]{1,2,0:T(4,128)(2,1)S(1)} all-gather(bf16[1,64,4]{1,2,0:T(4,128)(2,1)} %bitcast.879), channel_id=1, replica_groups=mesh['seq'=16,'head'=2] {'seq'}, dimensions={0}, use_global_device_ids=true | all-gather | bytes 8704 | tf_op jit(solution)/shard_map/all_gather | solution.py:251
  57.9 35.9 %all-gather.5 = bf16[16,64,4]{1,2,0:T(4,128)(2,1)S(1)} all-gather(bf16[1,64,4]{1,2,0:T(4,128)(2,1)} %bitcast.880), channel_id=1, replica_groups=mesh['seq'=16,'head'=2] {'seq'}, dimensions={0}, use_global_device_ids=true | all-gather | bytes 8704 | tf_op jit(solution)/shard_map/all_gather | solution.py:252
  100.9 24.5 %all-gather.23.cloned.1.call-done = bf16[1024,512]{1,0:T(8,128)(2,1)} async-done(((bf16[64,512]{1,0:T(8,128)(2,1)}), bf16[1024,512]{1,0:T(8,128)(2,1)}) %all-gather.23.cloned.1.call-update) | async-done | bytes 1048592 | tf_op jit(solution)/shard_map/all_gather | solution.py:247
  132.9 54.6 %all-gather.21.cloned.1.call-done = bf16[1024,1024]{1,0:T(8,128)(2,1)} async-done(((bf16[64,1024]{1,0:T(8,128)(2,1)}), bf16[1024,1024]{1,0:T(8,128)(2,1)}) %all-gather.21.cloned.1.call-update) | async-done | bytes 2097168 | tf_op jit(solution)/shard_map/all_gather | solution.py:249
  198.2 123.6 %while.128 = (s32[]{:T(128)}, f32[4,128,128]{2,1,0:T(8,128)}, f32[4,128,256]{2,1,0:T(8,128)S(1)}, f32[3,4,64,256]{3,2,1,0:T(8,128)}, f32[3,4,64,128]{3,2,0,1:T(8...) while((s32[]{:T(128)}, f32[4,128,128]{2,1,0:T(8,128)}, ...), condition=%wide.region_5.6_spmd.clone.clone, body=%wide.region_3.5_spmd.clone.clone.sunk | while | flops 806933568 | bytes 14639129 | solution.py:194
  202.2 20.3 custom-call.50
  243.3 20.3 custom-call.50
  284.5 20.3 custom-call.50
  329.5 55.2 %all-gather.35.cloned.1.call-done = bf16[64,128,128]{2,1,0:T(8,128)(2,1)} async-done(((bf16[4,128,128]{2,1,0:T(8,128)(2,1)}), bf16[64,128,128]{2,1,0:T(8,128)(2,1)}) %all-gather.35.cloned.1.call-update) | async-done | bytes 2097168 | tf_op jit(solution)/shard_map/all_gather | solution.py:25
  384.7 77.6 %all-gather.37.cloned.1.call-done = bf16[64,128,256]{2,1,0:T(8,128)(2,1)} async-done(((bf16[4,128,256]{2,1,0:T(8,128)(2,1)}), bf16[64,128,256]{2,1,0:T(8,128)(2,1)}) %all-gather.37.cloned.1.call-update) | async-done | bytes 4194320 | tf_op jit(solution)/shard_map/all_gather | solution.py:25
  466.0 58.1 %all-gather.27.cloned.1.call-done = bf16[1024,1024]{0,1:T(8,128)(2,1)} async-done(((bf16[1024,64]{0,1:T(8,128)(2,1)}), bf16[1024,1024]{0,1:T(8,128)(2,1)}) %all-gather.27.cloned.1.call-update) | async-done | bytes 2097168 | tf_op jit(solution)/shard_map/all_gather | solution.py:255
  547.9 66.8 %all-gather.29.cloned.1.call-done = bf16[1024,1408]{1,0:T(8,128)(2,1)} async-done(((bf16[64,1408]{1,0:T(8,128)(2,1)}), bf16[1024,1408]{1,0:T(8,128)(2,1)}) %all-gather.29.cloned.1.call-update) | async-done | bytes 2883600 | tf_op jit(solution)/shard_map/all_gather | solution.py:253
  618.5 63.6 %all-gather.31.cloned.1.call-done = bf16[1024,1408]{1,0:T(8,128)(2,1)} async-done(((bf16[64,1408]{1,0:T(8,128)(2,1)}), bf16[1024,1408]{1,0:T(8,128)(2,1)}) %all-gather.31.cloned.1.call-update) | async-done | bytes 2883600 | tf_op jit(solution)/shard_map/all_gather | solution.py:254
  685.8 63.7 %all-gather.33.cloned.1.call-done = bf16[1408,1024]{0,1:T(8,128)(2,1)} async-done(((bf16[1408,64]{0,1:T(8,128)(2,1)}), bf16[1408,1024]{0,1:T(8,128)(2,1)}) %all-gather.33.cloned.1.call-update) | async-done | bytes 2883600 | tf_op jit(solution)/shard_map/all_gather | solution.py:256
  793.6 47.0 %all-gather.39.cloned.1.call-done = bf16[64,128,128]{2,1,0:T(8,128)(2,1)} async-done(((bf16[4,128,128]{2,1,0:T(8,128)(2,1)}), bf16[64,128,128]{2,1,0:T(8,128)(2,1)}) %all-gather.39.cloned.1.call-update) | async-done | bytes 2097168 | tf_op jit(solution)/shard_map/all_gather | solution.py:45
  840.6 77.6 %all-gather.41.cloned.1.call-done = bf16[64,128,256]{2,1,0:T(8,128)(2,1)} async-done(((bf16[4,128,256]{2,1,0:T(8,128)(2,1)}), bf16[64,128,256]{2,1,0:T(8,128)(2,1)}) %all-gather.41.cloned.1.call-update) | async-done | bytes 4194320 | tf_op jit(solution)/shard_map/all_gather | solution.py:45
  918.3 25.2 %while.127 = (s32[]{:T(128)}, f32[4,128,256]{2,1,0:T(8,128)S(1)}, s32[]{:T(128)}, bf16[16,4,128,128]{3,2,1,0:T(8,128)(2,1)}, bf16[16,4,128,256]{3,2,1,0:T(8,128)...) while((s32[]{:T(128)}, f32[4,128,256]{2,1,0:T(8,128)S(1)}, s32[]{:T(128)}, ...), condition=%wide.region_16.17_spmd.clone, body=%wide.region_15.16_spmd.clone.sunk | while | flops 201981952 | bytes 3017381 | solution.py:63
  947.8 168.8 %while.126 = (s32[]{:T(128)}, f32[4,128,128]{2,1,0:T(8,128)S(1)}, f32[4,128,256]{2,1,0:T(8,128)S(1)}, f32[3,4,64,128]{3,2,0,1:T(8,128)}, f32[3,4,64,128]{3,2,0,1...) while((s32[]{:T(128)}, f32[4,128,128]{2,1,0:T(8,128)S(1)}, ...), condition=%wide.region_28.29_spmd.clone.clone, body=%wide.region_17.28_spmd.clone.clone.sunk | while | flops 1625209088 | bytes 30326172 | solution.py:194
  969.3 20.4 custom-call.49
  1025.5 20.4 custom-call.49
  1081.7 20.4 custom-call.49
  1166.7 80.5 %all-reduce.5 = (f32[4,512]{1,0:T(4,128)}, f32[4,512]{1,0:T(4,128)}, f32[4,1024]{1,0:T(4,128)}, f32[4]{0:T(128)}, f32[4]{0:T(128)}) all-reduce(f32[4,512]{1,0:T(4,128)S(1)} %pad_maximum_fusion.4, f32[4,512]{1,0:T(4,128)S(1)} %pad_maximum_fusion.5, f32[4,1024]{1,0:T(4,128)S(1)} %pad_maximum_fusion.3, ...), channel_id=1, replica_groups=mesh['seq'=16,'head'=2] {'seq'}, use_global_device_ids=true, to_apply=%region_45.46 | all-reduce | flops 8200 | bytes 65600 | tf_op jit(solution)/shard_map/psum | solution.py:373
  1248.5 38.0 %reduce-scatter.33.cloned.1.call-done = f32[64,4]{1,0:T(8,128)} async-done(((f32[1024,4]{1,0:T(8,128)}), f32[64,4]{1,0:T(8,128)}) %reduce-scatter.33.cloned.1.call-update) | async-done | bytes 1040
  1306.2 44.6 %all-reduce.4 = (f32[1024]{0:T(1024)}, f32[256]{0:T(256)}, f32[1024]{0:T(1024)}) all-reduce(f32[1024]{0:T(1024)S(1)} %get-tuple-element.2439, f32[256]{0:T(256)S(1)} %copy-done.82, f32[1024]{0:T(1024)S(1)} %copy-done.75), channel_id=1, replica_groups=mesh['seq'=16,'head'=2] {'seq','head'}, use_global_device_ids=true, to_apply=%region_34.35 | all-reduce | flops 2304 | bytes 18432 | tf_op jit(solution)/shard_map/psum | solution.py:376
  1353.5 51.4 %reduce-scatter.21.cloned.1.call-done = f32[64,1024]{1,0:T(8,128)} async-done(((f32[1024,1024]{1,0:T(8,128)}), f32[64,1024]{1,0:T(8,128)}) %reduce-scatter.21.cloned.1.call-update) | async-done | bytes 262160 | tf_op jit(solution)/shard_map/reduce_scatter | solution.py:383
  1404.9 97.6 %reduce-scatter.23.cloned.1.call-done = f32[1024,64]{0,1:T(8,128)} async-done(((f32[1024,1024]{0,1:T(8,128)}), f32[1024,64]{0,1:T(8,128)}) %reduce-scatter.23.cloned.1.call-update) | async-done | bytes 262160 | tf_op jit(solution)/shard_map/reduce_scatter | solution.py:386
  1502.5 128.3 %reduce-scatter.25.cloned.1.call-done = f32[64,1408]{1,0:T(8,128)} async-done(((f32[1024,1408]{1,0:T(8,128)}), f32[64,1408]{1,0:T(8,128)}) %reduce-scatter.25.cloned.1.call-update) | async-done | bytes 360464 | tf_op jit(solution)/shard_map/reduce_scatter | solution.py:387
  1630.9 129.9 %reduce-scatter.27.cloned.1.call-done = f32[64,1408]{1,0:T(8,128)} async-done(((f32[1024,1408]{1,0:T(8,128)}), f32[64,1408]{1,0:T(8,128)}) %reduce-scatter.27.cloned.1.call-update) | async-done | bytes 360464 | tf_op jit(solution)/shard_map/reduce_scatter | solution.py:388
  1760.8 129.9 %reduce-scatter.29.cloned.1.call-done = f32[1408,64]{0,1:T(8,128)} async-done(((f32[1408,1024]{0,1:T(8,128)}), f32[1408,64]{0,1:T(8,128)}) %reduce-scatter.29.cloned.1.call-update) | async-done | bytes 360464 | tf_op jit(solution)/shard_map/reduce_scatter | solution.py:389
  1890.7 85.4 %reduce-scatter.15.cloned.1.call-done = f32[64,512]{1,0:T(8,128)} async-done(((f32[1024,512]{1,0:T(8,128)}), f32[64,512]{1,0:T(8,128)}) %reduce-scatter.15.cloned.1.call-update) | async-done | bytes 131088 | tf_op jit(solution)/shard_map/reduce_scatter | solution.py:380
  1976.2 80.7 %reduce-scatter.17.cloned.1.call-done = f32[64,512]{1,0:T(8,128)} async-done(((f32[1024,512]{1,0:T(8,128)}), f32[64,512]{1,0:T(8,128)}) %reduce-scatter.17.cloned.1.call-update) | async-done | bytes 131088 | tf_op jit(solution)/shard_map/reduce_scatter | solution.py:381
  2056.8 94.8 %reduce-scatter.19.cloned.1.call-done = f32[64,1024]{1,0:T(8,128)} async-done(((f32[1024,1024]{1,0:T(8,128)}), f32[64,1024]{1,0:T(8,128)}) %reduce-scatter.19.cloned.1.call-update) | async-done | bytes 262160 | tf_op jit(solution)/shard_map/reduce_scatter | solution.py:382
  (689 shorter events, 389.9 us)
Async XLA Ops:
  7.2 88.1 %all-gather.19.cloned.1.call-start = ((), (), s32[]{:S(2)}) async-start(), calls=%async_computation.10 | async-start | bytes 1114112 | tf_op jit(solution)/shard_map/all_gather | solution.py:248
  8.0 117.5 %all-gather.23.cloned.1.call-start = ((), (), s32[]{:S(2)}) async-start(), calls=%async_computation.12 | async-start | bytes 1114112 | tf_op jit(solution)/shard_map/all_gather | solution.py:247
  8.7 178.7 %all-gather.21.cloned.1.call-start = ((), (), s32[]{:S(2)}) async-start(), calls=%async_computation.11 | async-start | bytes 2228224 | tf_op jit(solution)/shard_map/all_gather | solution.py:249
  9.5 315.6 %all-gather.25.cloned.1.call-start = ((), (), s32[]{:S(2)}) async-start(), calls=%async_computation.13 | async-start | bytes 2228224 | tf_op jit(solution)/shard_map/all_gather | solution.py:250
  10.0 374.6 %all-gather.35.cloned.1.call-start = ((), (), s32[]{:S(2)}) async-start(), calls=%async_computation.28 | async-start | bytes 2228224 | tf_op jit(solution)/shard_map/all_gather | solution.py:25
  97.1 33.4 %collective-permute-start = (bf16[3,512]{1,0:T(4,128)(2,1)S(1)}, bf16[3,512]{1,0:T(4,128)(2,1)S(1)}, u32[]{:S(2)}, u32[]{:S(2)}) collective-permute-start(bf16[3,512]{1,0:T(4,128)(2,1)S(1)} %slice.229), channel_id=1, source_target_pairs={{0,2},{2,4},{4,6},{6,8},{8,10},{10,12},{12,14},{14,16},{16,18},{18... | collective-permute-start | bytes 9224 | tf_op jit(solution)/shard_map/ppermute | solution.py:19
  127.1 4.7 collective-permute-start.2
  189.7 4.5 collective-permute-start.1
  323.4 138.9 %all-gather.37.cloned.1.call-start = ((), (), s32[]{:S(2)}) async-start(), calls=%async_computation.29 | async-start | bytes 4456448 | tf_op jit(solution)/shard_map/all_gather | solution.py:25
  324.2 199.9 %all-gather.27.cloned.1.call-start = ((), (), s32[]{:S(2)}) async-start(), calls=%async_computation.14 | async-start | bytes 2228224 | tf_op jit(solution)/shard_map/all_gather | solution.py:255
  325.0 219.8 %all-reduce.11.cloned.1.call-start = ((), (), s32[]{:S(2)}) async-start(), calls=%async_computation.15 | async-start | bytes 786432 | tf_op jit(solution)/shard_map/psum | solution.py:287
  465.0 316.7 %copy-start.4 = (f32[4,192,256]{2,1,0:T(8,128)}, f32[4,192,256]{2,1,0:T(8,128)S(1)}, u32[]{:S(2)}) copy-start(f32[4,192,256]{2,1,0:T(8,128)S(1)} %get-tuple-element.2698) | copy-start | bytes 2359300
  527.4 87.3 %all-gather.29.cloned.1.call-start = ((), (), s32[]{:S(2)}) async-start(), calls=%async_computation.16 | async-start | bytes 3063808 | tf_op jit(solution)/shard_map/all_gather | solution.py:253
  528.2 153.9 %all-gather.31.cloned.1.call-start = ((), (), s32[]{:S(2)}) async-start(), calls=%async_computation.17 | async-start | bytes 3063808 | tf_op jit(solution)/shard_map/all_gather | solution.py:254
  528.8 220.7 %all-gather.33.cloned.1.call-start = ((), (), s32[]{:S(2)}) async-start(), calls=%async_computation.18 | async-start | bytes 3063808 | tf_op jit(solution)/shard_map/all_gather | solution.py:256
  529.5 246.2 %all-reduce.13.cloned.1.call-start = ((), (), s32[]{:S(2)}) async-start(), calls=%async_computation.19 | async-start | bytes 786432 | tf_op jit(solution)/shard_map/psum | solution.py:307
  758.4 82.2 %all-gather.39.cloned.1.call-start = ((), (), s32[]{:S(2)}) async-start(), calls=%async_computation.30 | async-start | bytes 2228224 | tf_op jit(solution)/shard_map/all_gather | solution.py:45
  760.3 158.0 %all-gather.41.cloned.1.call-start = ((), (), s32[]{:S(2)}) async-start(), calls=%async_computation.31 | async-start | bytes 4456448 | tf_op jit(solution)/shard_map/all_gather | solution.py:45
  784.7 462.4 %reduce-scatter.31.cloned.1.call-start = ((), (), s32[]{:S(2)}) async-start(), calls=%async_computation.32 | async-start | bytes 557056
  1120.4 8.9 collective-permute-start.3
  1122.8 8.5 collective-permute-start.4
  1125.0 8.5 collective-permute-start.5
  1128.0 158.5 %reduce-scatter.33.cloned.1.call-start = ((), (), s32[]{:S(2)}) async-start(), calls=%async_computation.33 | async-start | bytes 557056
  1129.3 175.5 %all-reduce.15.cloned.1.call-start = ((), (), s32[]{:S(2)}) async-start(), calls=%async_computation.34 | async-start | bytes 1572864 | tf_op jit(solution)/shard_map/psum | solution.py:295
  1138.2 266.8 %reduce-scatter.21.cloned.1.call-start = ((), (), s32[]{:S(2)}) async-start(), calls=%async_computation.23 | async-start | bytes 4456448 | tf_op jit(solution)/shard_map/reduce_scatter | solution.py:383
  1141.1 361.5 %reduce-scatter.23.cloned.1.call-start = ((), (), s32[]{:S(2)}) async-start(), calls=%async_computation.24 | async-start | bytes 4456448 | tf_op jit(solution)/shard_map/reduce_scatter | solution.py:386
  1145.4 485.5 %reduce-scatter.25.cloned.1.call-start = ((), (), s32[]{:S(2)}) async-start(), calls=%async_computation.25 | async-start | bytes 6127616 | tf_op jit(solution)/shard_map/reduce_scatter | solution.py:387
  1150.1 610.8 %reduce-scatter.27.cloned.1.call-start = ((), (), s32[]{:S(2)}) async-start(), calls=%async_computation.26 | async-start | bytes 6127616 | tf_op jit(solution)/shard_map/reduce_scatter | solution.py:388
  1154.6 736.2 %reduce-scatter.29.cloned.1.call-start = ((), (), s32[]{:S(2)}) async-start(), calls=%async_computation.27 | async-start | bytes 6127616 | tf_op jit(solution)/shard_map/reduce_scatter | solution.py:389
  1159.1 817.0 %reduce-scatter.15.cloned.1.call-start = ((), (), s32[]{:S(2)}) async-start(), calls=%async_computation.20 | async-start | bytes 2228224 | tf_op jit(solution)/shard_map/reduce_scatter | solution.py:380
  1161.1 895.7 %reduce-scatter.17.cloned.1.call-start = ((), (), s32[]{:S(2)}) async-start(), calls=%async_computation.21 | async-start | bytes 2228224 | tf_op jit(solution)/shard_map/reduce_scatter | solution.py:381
  1163.0 988.6 %reduce-scatter.19.cloned.1.call-start = ((), (), s32[]{:S(2)}) async-start(), calls=%async_computation.22 | async-start | bytes 4456448 | tf_op jit(solution)/shard_map/reduce_scatter | solution.py:382
  (102 other events, 2029.1 us)
Sparse Core Ops, SparseCore 0:
  10.8 57.8 all-gather.18
  71.4 53.9 all-gather.22
  128.2 59.2 all-gather.20
  190.1 60.0 all-gather.24
  323.5 61.0 all-gather.34
  387.9 74.3 all-gather.36
  465.1 58.9 all-gather.26
  527.6 17.1 all-reduce.10
  547.6 67.1 all-gather.28
  617.4 64.6 all-gather.30
  684.8 64.6 all-gather.32
  758.6 17.0 all-reduce.12
  779.0 61.5 all-gather.38
  843.8 74.3 all-gather.40
  1128.1 82.2 reduce-scatter.30
  1212.5 73.9 reduce-scatter.32
  1289.3 15.4 all-reduce.14
  1307.6 97.3 reduce-scatter.20
  1407.8 94.7 reduce-scatter.22
  1505.3 125.5 reduce-scatter.24
  1633.8 126.9 reduce-scatter.26
  1763.7 126.9 reduce-scatter.28
  1893.6 82.5 reduce-scatter.14
  1978.9 77.9 reduce-scatter.16
  2059.7 91.8 reduce-scatter.18
where the time goes:
time: 2170 us; the launch traced here: 2160 us
  waiting for transfers between devices  1480 us (68%)
  matrix products  220 us (10%)
  blocking collectives  204 us (9%)
  other arithmetic  175 us (8%)
  local copies, waits for them, and re-layouts  46.6 us (2%)
    all_gather x2, waiting for transfers between devices, prefix(): lax.all_gather(a.astype(kind), axis)  133 us
    reduce_scatter x1, waiting for transfers between devices, shards(): lax.psum_scatter(grad_ffup, 'seq', scatter_dimension=0, tiled=True)  130 us
    reduce_scatter x1, waiting for transfers between devices, shards(): lax.psum_scatter(grad_ffdown, 'seq', scatter_dimension=1, tiled=True)  130 us
    reduce_scatter x1, waiting for transfers between devices, shards(): lax.psum_scatter(grad_ffgate, 'seq', scatter_dimension=0, tiled=True)  128 us
    another operation x30, other arithmetic, span_terms(): lax.linalg.triangular_solve(lower, rhs, left_side=True, lower=True, unit_...  128 us
    all_gather x2, waiting for transfers between devices, entering(): lax.all_gather(part.astype(kind), axis)  125 us
    reduce_scatter x1, waiting for transfers between devices, shards(): lax.psum_scatter(grad_out, 'seq', scatter_dimension=1, tiled=True)  97.6 us
    reduce_scatter x1, waiting for transfers between devices, shards(): lax.psum_scatter(grad_value, 'seq', scatter_dimension=0, tiled=True)  94.8 us
  transfers between devices with their start and end apart: 31, of which 24 were waited for; matrix products, arithmetic and copies ran while one was open for 10% of the time, Pallas kernels for 0%

commit v1 on v0

v1 whole, which is shorter than its diff:
```python
import functools

import jax
import jax.numpy as jnp
from jax import lax
from jax.experimental import pallas as pl
from jax.experimental.pallas import tpu as pltpu
from jax.sharding import PartitionSpec as P

CONV = 4
SPAN = 64


EPS_NORM = 1e-06
EPS_HEAD = 1e-05
EPS_UNIT = 1e-06


def from_behind(block, axis, distance):
    devices = range(lax.axis_size(axis))
    route = [(i - distance, i) for i in devices if i - distance in devices]
    return lax.ppermute(block, axis, route)


def pair_sum(block):
    return block + lax.ppermute(block, "head", [(0, 1), (1, 0)])


def matmul(left, right):
    return jnp.dot(left, right, preferred_element_type=jnp.float32)


def matmul_tl(left, right):
    return lax.dot_general(
        left, right, (((0,), (0,)), ((), ())), preferred_element_type=jnp.float32
    )


def matmul_tr(left, right):
    return lax.dot_general(
        left, right, (((1,), (1,)), ((), ())), preferred_element_type=jnp.float32
    )


def rms_scale(values):
    return lax.rsqrt(jnp.mean(values * values, axis=-1, keepdims=True) + EPS_NORM)


def norm_gradient_step(unit_input_gradient, unit_input, inverse_scale):
    return inverse_scale * (
        unit_input_gradient
        - unit_input * jnp.mean(unit_input_gradient * unit_input, axis=-1, keepdims=True)
    )


def conv_apply(extended, weight, rows):
    total = weight[0] * extended[0:rows]
    for tap in range(1, CONV):
        total = total + weight[tap] * extended[tap : tap + rows]
    return total


def conv_back_apply(extended, weight, rows):
    total = weight[0] * extended[CONV - 1 : CONV - 1 + rows]
    for tap in range(1, CONV):
        total = total + weight[tap] * extended[CONV - 1 - tap : CONV - 1 - tap + rows]
    return total


def conv_weight_grad(grad_out, extended, rows):
    return jnp.stack(
        [jnp.sum(grad_out * extended[tap : tap + rows], axis=0) for tap in range(CONV)], axis=0
    )


def prepare(qc, kc, vc, b_lin, a_lin, a_log, dt_bias):
    heads = a_log.shape[0]
    rows = qc.shape[0]
    q_act = jax.nn.silu(qc).reshape(rows, heads, -1)
    k_act = jax.nn.silu(kc).reshape(rows, heads, -1)
    dim_k = q_act.shape[-1]
    query = (
        q_act
        * lax.rsqrt(jnp.sum(q_act * q_act, axis=-1, keepdims=True) + EPS_UNIT)
        * dim_k ** (-0.5)
    )
    keyvec = k_act * lax.rsqrt(jnp.sum(k_act * k_act, axis=-1, keepdims=True) + EPS_UNIT)
    value = jax.nn.silu(vc).reshape(rows, heads, -1)
    beta = jax.nn.sigmoid(b_lin).T
    logdec = (-jnp.exp(a_log)[None, :] * jax.nn.softplus(a_lin + dt_bias[None, :])).T
    return (
        jnp.transpose(query, (1, 0, 2)),
        jnp.transpose(keyvec, (1, 0, 2)),
        jnp.transpose(value, (1, 0, 2)),
        beta,
        logdec,
    )


def finish(block_result, gate_pre, out_gain):
    heads, rows, dim_v = block_result.shape
    normed = (
        block_result
        * lax.rsqrt(jnp.mean(block_result * block_result, axis=-1, keepdims=True) + EPS_HEAD)
        * out_gain
    )
    gating = jax.nn.silu(gate_pre).reshape(rows, heads, dim_v)
    return (jnp.transpose(normed, (1, 0, 2)) * gating).reshape(rows, heads * dim_v)


def halves(x):
    high = x.astype(jnp.bfloat16)
    return high, (x - high.astype(jnp.float32)).astype(jnp.bfloat16)


def raw_dot(a, b, ca, cb):
    a_high, a_low = halves(a)
    b_high, b_low = halves(b)

    def one(x, y):
        return lax.dot_general(
            x, y, (((ca,), (cb,)), ((), ())), preferred_element_type=jnp.float32
        )

    return one(a_high, b_high) + (one(a_high, b_low) + one(a_low, b_high))


@functools.partial(jax.custom_vjp, nondiff_argnums=(2, 3))
def dot(a, b, ca, cb):
    return raw_dot(a, b, ca, cb)


def dot_fwd(a, b, ca, cb):
    return raw_dot(a, b, ca, cb), (a, b)


def dot_bwd(ca, cb, kept, g):
    a, b = kept
    da = raw_dot(g, b, 1, 1 - cb) if ca == 1 else raw_dot(b, g, 1 - cb, 1)
    db = raw_dot(a, g, 1 - ca, 0) if cb == 0 else raw_dot(g, a, 0, 1 - ca)
    return da, db


dot.defvjp(dot_fwd, dot_bwd)


def raw_inverse(lower):
    size = lower.shape[0]
    row = lax.broadcasted_iota(jnp.int32, (size, size), 0)
    col = lax.broadcasted_iota(jnp.int32, (size, size), 1)
    result = jnp.where(row == col, 1.0, 0.0)
    width = 1
    while width < size:
        inside = (row // (2 * width) == col // (2 * width)) & (row // width != col // width)
        band = jnp.where(inside, lower, 0.0)
        if width == 1:
            result = result - band
        else:
            result = result - raw_dot(result, raw_dot(band, result, 1, 0), 1, 0)
        width = 2 * width
    return result


@jax.custom_vjp
def inverse(lower):
    return raw_inverse(lower)


def inverse_fwd(lower):
    result = raw_inverse(lower)
    return result, result


def inverse_bwd(result, g):
    return (-raw_dot(raw_dot(result, g, 0, 0), result, 1, 1),)


inverse.defvjp(inverse_fwd, inverse_bwd)


def span_terms(query, keyvec, value, beta, log_col, log_row):
    size, dim_k = query.shape
    row = lax.broadcasted_iota(jnp.int32, (size, size), 0)
    col = lax.broadcasted_iota(jnp.int32, (size, size), 1)
    strict = row > col
    weak = row >= col
    cum_col = jnp.sum(jnp.where(weak, log_row, 0.0), axis=1, keepdims=True)
    cum_row = jnp.sum(jnp.where(row <= col, log_col, 0.0), axis=0, keepdims=True)
    total = jnp.sum(log_col, axis=0, keepdims=True)
    after = jnp.sum(jnp.where(row < col, log_row, 0.0), axis=1, keepdims=True)
    decay = jnp.where(weak, jnp.exp(jnp.where(weak, cum_col - cum_row, 0.0)), 0.0)
    kk = dot(keyvec, keyvec, 1, 1)
    solver = inverse(jnp.where(strict, beta * decay * kk, 0.0))
    reach = jnp.exp(cum_col)
    starting_value = dot(solver, beta * value, 1, 0)
    mixk = dot(solver, (beta * reach) * keyvec, 1, 0)
    scores = dot(query, keyvec, 1, 1) * decay
    empty_output = dot(scores, starting_value, 1, 0)
    extent = reach * query - dot(scores, mixk, 1, 0)
    trailing = jnp.exp(after) * keyvec
    k_row = lax.broadcasted_iota(jnp.int32, (dim_k, dim_k), 0)
    k_col = lax.broadcasted_iota(jnp.int32, (dim_k, dim_k), 1)
    state_matrix = jnp.where(k_row == k_col, jnp.exp(total), 0.0) - dot(trailing, mixk, 0, 0)
    addend = dot(trailing, starting_value, 0, 0)
    return empty_output, extent, state_matrix, addend


def spans_kernel(q, k, v, b, lc, lr, empty, extent, matrix, addend, product, running):
    heads, dim_k = q.shape[1], q.shape[3]

    @pl.when(pl.program_id(0) == 0)
    def _():
        k_row = lax.broadcasted_iota(jnp.int32, (dim_k, dim_k), 0)
        k_col = lax.broadcasted_iota(jnp.int32, (dim_k, dim_k), 1)
        for h in range(heads):
            product[h] = jnp.where(k_row == k_col, 1.0, 0.0)
            running[h] = jnp.zeros(running.shape[1:], jnp.float32)

    for h in range(heads):
        e, x, m, a = span_terms(q[0, h], k[0, h], v[0, h], b[0, h], lc[0, h], lr[0, h])
        empty[0, h] = e
        extent[0, h] = x
        matrix[0, h] = m
        addend[0, h] = a
        product[h] = raw_dot(m, product[h], 1, 0)
        running[h] = raw_dot(m, running[h], 1, 0) + a


def apply_kernel(empty, extent, matrix, addend, start, out, states, state):
    heads = empty.shape[1]

    @pl.when(pl.program_id(0) == 0)
    def _():
        state[...] = start[...]

    for h in range(heads):
        s = state[h]
        states[0, h] = s
        out[0, h] = empty[0, h] + raw_dot(extent[0, h], s, 1, 0)
        state[h] = raw_dot(matrix[0, h], s, 1, 0) + addend[0, h]


def partial_kernel(extent, matrix, grad, result):
    heads = extent.shape[1]

    @pl.when(pl.program_id(0) == 0)
    def _():
        result[...] = jnp.zeros(result.shape, jnp.float32)

    for h in range(heads):
        result[h] = raw_dot(matrix[0, h], result[h], 0, 0) + raw_dot(
            extent[0, h], grad[0, h], 0, 0
        )


def back_kernel(
    q, k, v, b, lc, lr, extent, matrix, states, grad, end, dq, dk, dv, db, dlc, dlr, later
):
    heads = q.shape[1]

    @pl.when(pl.program_id(0) == 0)
    def _():
        later[...] = end[...]

    for h in range(heads):
        g_state = later[h]
        g_out = grad[0, h]
        s = states[0, h]
        args = (q[0, h], k[0, h], v[0, h], b[0, h], lc[0, h], lr[0, h])
        _, back = jax.vjp(span_terms, *args)
        d = back((g_out, raw_dot(g_out, s, 1, 1), raw_dot(g_state, s, 1, 1), g_state))
        for ref, part in zip((dq, dk, dv, db, dlc, dlr), d):
            ref[0, h] = part
        later[h] = raw_dot(matrix[0, h], g_state, 0, 0) + raw_dot(extent[0, h], g_out, 0, 0)


def chain_kernel(reverse, matrices, addends, out):
    n = matrices.shape[0]

    def turn(i, state):
        at = n - 1 - i if reverse else i
        out[at] = state
        return raw_dot(matrices[at], state, 0 if reverse else 1, 0) + addends[at]

    lax.fori_loop(0, n, turn, jnp.zeros(out.shape[1:], jnp.float32))


def shape_of(array):
    return jax.ShapeDtypeStruct(array.shape, jnp.float32)


def over_blocks(kernel, blocks, whole_in, outs, whole_out, scratch, reverse, *arrays):
    def spec(shape, whole):
        rank = len(shape)
        if whole:
            return pl.BlockSpec(shape, lambda c: (0,) * rank)
        if reverse:
            return pl.BlockSpec((1,) + shape[1:], lambda c: (blocks - 1 - c,) + (0,) * (rank - 1))
        return pl.BlockSpec((1,) + shape[1:], lambda c: (c,) + (0,) * (rank - 1))

    cut = len(arrays) - whole_in
    return pl.pallas_call(
        kernel,
        grid=(blocks,),
        in_specs=[spec(a.shape, i >= cut) for i, a in enumerate(arrays)],
        out_specs=[spec(s, i >= len(outs) - whole_out) for i, s in enumerate(outs)],
        out_shape=[jax.ShapeDtypeStruct(s, jnp.float32) for s in outs],
        scratch_shapes=[pltpu.VMEM(s, jnp.float32) for s in scratch],
        compiler_params=pltpu.CompilerParams(
            dimension_semantics=("arbitrary",), vmem_limit_bytes=48 * 1024 * 1024
        ),
    )(*arrays)


def chain(matrices, addends, reverse):
    return pl.pallas_call(
        functools.partial(chain_kernel, reverse),
        out_shape=shape_of(addends),
        compiler_params=pltpu.CompilerParams(vmem_limit_bytes=48 * 1024 * 1024),
    )(matrices, addends)


def by_block(array):
    heads, rows = array.shape[:2]
    return jnp.swapaxes(array.reshape((heads, rows // SPAN, SPAN) + array.shape[2:]), 0, 1)


def by_head(array):
    blocks, heads, span = array.shape[:3]
    return jnp.swapaxes(array, 0, 1).reshape((heads, blocks * span) + array.shape[3:])


def exchange(parts):
    return lax.all_to_all(parts, "seq", 0, 0)


def columns_out(array, n):
    heads, rows, cols = array.shape
    parts = n // heads
    return (
        array.reshape(heads, rows, parts, cols // parts)
        .transpose(0, 2, 1, 3)
        .reshape(n, rows, cols // parts)
    )


def columns_in(array, heads):
    n, rows, width = array.shape
    parts = n // heads
    return (
        array.reshape(heads, parts, rows, width)
        .transpose(0, 2, 1, 3)
        .reshape(heads, rows, parts * width)
    )


def shards(
    block_in,
    first_norm_gain,
    w_query,
    w_key,
    w_value,
    w_gate,
    w_alpha,
    w_beta,
    conv_query,
    conv_key,
    conv_value,
    a_log,
    dt_bias,
    out_gain,
    w_out,
    second_norm_gain,
    w_ffgate,
    w_ffup,
    w_ffdown,
    cotangent,
):
    rows = block_in.shape[0]
    edge = CONV - 1
    n = lax.axis_size("seq")
    heads = a_log.shape[0]
    blocks = rows // SPAN
    width_k = w_query.shape[1]
    width_v = w_value.shape[1]
    width_f = w_ffgate.shape[1]
    width_m = 2 * width_k + width_v
    width_g = width_m + width_v

    def gather(*parts):
        return lax.all_gather(jnp.concatenate(parts, axis=1), "seq", axis=0, tiled=True)

    full_in = gather(w_query, w_key, w_value, w_gate, w_alpha, w_beta)
    full_o = gather(w_out.T)
    full_ff = gather(w_ffgate, w_ffup)
    full_fd = gather(w_ffdown.T)
    input_float = block_in.astype(jnp.float32)
    first_inverse_scale = rms_scale(input_float)
    first_unit_input = input_float * first_inverse_scale
    first_normed_input = (first_unit_input * first_norm_gain).astype(jnp.bfloat16)
    projected = matmul(first_normed_input, full_in)
    mix_pre = projected[:, :width_m].astype(jnp.bfloat16)
    gpre = projected[:, width_m:width_g].astype(jnp.bfloat16)
    a_lin = projected[:, width_g : width_g + heads]
    b_lin = projected[:, width_g + heads :]
    mix_taps = jnp.concatenate([conv_query, conv_key, conv_value], axis=1)
    before = from_behind(mix_pre[rows - edge :], "seq", 1)
    mix_ext = jnp.concatenate([before, mix_pre], axis=0).astype(jnp.float32)
    mixc = conv_apply(mix_ext, mix_taps, rows)
    prepared, prepare_back = jax.vjp(
        prepare,
        mixc[:, :width_k],
        mixc[:, width_k : 2 * width_k],
        mixc[:, 2 * width_k :],
        b_lin,
        a_lin,
        a_log,
        dt_bias,
    )
    query, keyvec, value = (by_block(a) for a in prepared[:3])
    beta, log_col = (by_block(a)[..., None] for a in prepared[3:])
    log_row = by_block(prepared[4])[:, :, None, :]
    items = (query, keyvec, value, beta, log_col, log_row)
    dim_k, dim_v = query.shape[-1], value.shape[-1]
    shape_k, shape_v = query.shape, value.shape
    shape_m = (blocks, heads, dim_k, dim_k)
    shape_s = (blocks, heads, dim_k, dim_v)
    empty, extent, matrix, addend, product, running = over_blocks(
        spans_kernel,
        blocks,
        0,
        (shape_v, shape_k, shape_m, shape_s, shape_m[1:], shape_s[1:]),
        2,
        (),
        False,
        *items,
    )
    parts = n // heads
    sent_matrices = jnp.broadcast_to(
        product[:, None], (heads, parts, dim_k, dim_k)
    ).reshape(n, dim_k, dim_k)
    matrices = exchange(sent_matrices)
    addends = exchange(columns_out(running, n))
    incoming = columns_in(exchange(chain(matrices, addends, False)), heads)
    block_result, states = over_blocks(
        apply_kernel,
        blocks,
        1,
        (shape_v, shape_s),
        0,
        (shape_s[1:],),
        False,
        empty,
        extent,
        matrix,
        addend,
        incoming,
    )
    on_f, finish_back = jax.vjp(finish, by_head(block_result), gpre.astype(jnp.float32), out_gain)
    on_b = on_f.astype(jnp.bfloat16)
    hidden_residual = input_float + pair_sum(matmul_tr(on_b, full_o))
    second_inverse_scale = rms_scale(hidden_residual)
    second_unit_input = hidden_residual * second_inverse_scale
    second_normed_input = (second_unit_input * second_norm_gain).astype(jnp.bfloat16)
    both = matmul(second_normed_input, full_ff)
    fg, fu = both[:, :width_f], both[:, width_f:]
    hid = (jax.nn.silu(fg) * fu).astype(jnp.bfloat16)
    fed = pair_sum(matmul_tr(hid, full_fd))
    block_out = (hidden_residual + fed).astype(jnp.bfloat16)
    feedforward_output_gradient = cotangent.astype(jnp.float32)
    dhid = matmul(cotangent, full_fd)
    sig = jax.nn.sigmoid(fg)
    dfu = (dhid * fg * sig).astype(jnp.bfloat16)
    dfg = (dhid * fu * sig * (1.0 + fg * (1.0 - sig))).astype(jnp.bfloat16)
    dboth = jnp.concatenate([dfg, dfu], axis=1)
    second_normed_gradient = pair_sum(matmul_tr(dboth, full_ff))
    second_norm_piece = jnp.sum(second_normed_gradient * second_unit_input, axis=0)
    hidden_gradient = feedforward_output_gradient + norm_gradient_step(
        second_normed_gradient * second_norm_gain, second_unit_input, second_inverse_scale
    )
    dh_b = hidden_gradient.astype(jnp.bfloat16)
    don = matmul(dh_b, full_o)
    output_gradient, dgpre, outgain_part = finish_back(don)
    outgain_part = pair_sum(outgain_part)
    output_gradient = by_block(output_gradient)
    (partial_gradient,) = over_blocks(
        partial_kernel, blocks, 0, (shape_s[1:],), 1, (), True, extent, matrix, output_gradient
    )
    behind = exchange(columns_out(partial_gradient, n))
    final_state_gradient = columns_in(exchange(chain(matrices, behind, True)), heads)

    def scatter(grad):
        return lax.psum_scatter(
            grad.astype(jnp.bfloat16), "seq", scatter_dimension=0, tiled=True
        ).astype(jnp.float32)

    dgb = dgpre.astype(jnp.bfloat16)
    sum_ffgate, sum_ffup = jnp.split(scatter(matmul_tl(second_normed_input, dboth)), 2, axis=1)
    sum_ffdown = scatter(matmul_tl(cotangent, hid)).T
    sum_out = scatter(matmul_tl(dh_b, on_b)).T
    sum_gate = scatter(matmul_tl(first_normed_input, dgb))
    grads = over_blocks(
        back_kernel,
        blocks,
        1,
        tuple(a.shape for a in items),
        0,
        (shape_s[1:],),
        True,
        *items,
        extent,
        matrix,
        states,
        output_gradient,
        final_state_gradient,
    )
    dq, dk, dv, dbeta, dlog_col, dlog_row = grads
    dlog = dlog_col[..., 0] + dlog_row[:, :, 0, :]
    grads_prepared = tuple(by_head(a) for a in (dq, dk, dv, dbeta[..., 0], dlog))
    dqc, dkc, dvc, db_lin, da_lin, alog_part, dt_part = prepare_back(grads_prepared)
    dmixc = jnp.concatenate([dqc, dkc, dvc], axis=1)
    after = from_behind(dmixc[:edge], "seq", -1)
    conv_part = conv_weight_grad(dmixc, mix_ext, rows)
    dmix = conv_back_apply(jnp.concatenate([dmixc, after], axis=0), mix_taps, rows)
    dcat = jnp.concatenate(
        [
            dmix.astype(jnp.bfloat16),
            dgb,
            da_lin.astype(jnp.bfloat16),
            db_lin.astype(jnp.bfloat16),
        ],
        axis=1,
    )
    dlate = jnp.concatenate([dcat[:, :width_m], dcat[:, width_g:]], axis=1)
    sum_late = scatter(matmul_tl(first_normed_input, dlate))
    sum_query = sum_late[:, :width_k]
    sum_key = sum_late[:, width_k : 2 * width_k]
    sum_value = sum_late[:, 2 * width_k : width_m]
    sum_alpha = sum_late[:, width_m : width_m + heads]
    sum_beta = sum_late[:, width_m + heads :]
    first_normed_gradient = pair_sum(matmul_tr(dcat, full_in))
    first_norm_piece = jnp.sum(first_normed_gradient * first_unit_input, axis=0)
    input_gradient = hidden_gradient + norm_gradient_step(
        first_normed_gradient * first_norm_gain, first_unit_input, first_inverse_scale
    )
    (
        grad_alog,
        grad_dt,
        grad_conv,
        first_norm_gain_gradient,
        second_norm_gain_gradient,
        grad_outgain,
    ) = lax.psum(
        (alog_part, dt_part, conv_part, first_norm_piece, second_norm_piece, outgain_part), "seq"
    )
    grad_convq = grad_conv[:, :width_k]
    grad_convk = grad_conv[:, width_k : 2 * width_k]
    grad_convv = grad_conv[:, 2 * width_k :]
    return (
        block_out,
        input_gradient,
        first_norm_gain_gradient,
        sum_query,
        sum_key,
        sum_value,
        sum_gate,
        sum_alpha,
        sum_beta,
        grad_convq,
        grad_convk,
        grad_convv,
        grad_alog,
        grad_dt,
        grad_outgain,
        sum_out,
        second_norm_gain_gradient,
        sum_ffgate,
        sum_ffup,
        sum_ffdown,
    )


def solution(mesh):
    placed = (
        P("seq", None),
        P(),
        P("seq", "head"),
        P("seq", "head"),
        P("seq", "head"),
        P("seq", "head"),
        P("seq", "head"),
        P("seq", "head"),
        P(None, "head"),
        P(None, "head"),
        P(None, "head"),
        P("head"),
        P("head"),
        P(),
        P("head", "seq"),
        P(),
        P("seq", "head"),
        P("seq", "head"),
        P("head", "seq"),
        P("seq", None),
    )
    return jax.shard_map(
        shards,
        mesh=mesh,
        in_specs=placed,
        out_specs=(
            P("seq", None),
            P("seq", None),
            P(),
            P("seq", "head"),
            P("seq", "head"),
            P("seq", "head"),
            P("seq", "head"),
            P("seq", "head"),
            P("seq", "head"),
            P(None, "head"),
            P(None, "head"),
            P(None, "head"),
            P("head"),
            P("head"),
            P(),
            P("head", "seq"),
            P(),
            P("seq", "head"),
            P("seq", "head"),
            P("head", "seq"),
        ),
        check_vma=False,
    )
```

time: 2170 us -> 866 us (0.40)
  waiting for transfers between devices: 1480 us -> 470 us
  matrix products: 220 us -> 42.2 us
  other arithmetic: 175 us -> 25.6 us
  Pallas kernels: 0 us -> 73.2 us
  blocking collectives: 204 us -> 147 us
    reduce_scatter x8 -> x4, waiting for transfers between devices: 798 us -> 219 us  [scatter(): lax.psum_scatter(grad.astype(jnp.bfloat16), 'seq', scatter_dimension=0, t...]
    all_gather x12 -> x4, waiting for transfers between devices: 589 us -> 176 us  [gather(): lax.all_gather(jnp.concatenate(parts, axis=1), 'seq', axis=0, tiled=True)]
    dot_general x113 -> x0, matrix products: 139 us -> none  [the longest x16 23.9 us: compose(): jnp.einsum('hij,hjk->hik', later[0], earlier[1], precision=MATMUL_ACCURACY)]
    another operation x58 -> x1, other arithmetic: 130 us -> 1.04 us  [the longest x30 128 us: span_terms(): lax.linalg.triangular_solve(lower, rhs, left_side=True, lower=True, unit_...]
    all_gather x2 -> x0, blocking collectives: 78.6 us -> none  [the longest x1 42.8 us: shards(): lax.all_gather(w_alpha, 'seq', axis=0, tiled=True)]
    pallas_call x0 -> x6, Pallas kernels: none -> 73.2 us  [the longest x4 67.1 us: over_blocks(): pl.pallas_call(kernel, grid=(blocks,), in_specs=[spec(a.shape, i >= cut)...]
    all_to_all x0 -> x3, blocking collectives: none -> 73 us  [exchange(): return lax.all_to_all(parts, 'seq', 0, 0)]
    psum x2 -> x1, blocking collectives: 125 us -> 74 us  [shards(): lax.psum((alog_part, dt_part, conv_part, first_norm_piece, second_norm_pi...]
  transfers between devices with their start and end apart: 31 -> 18, of which waited for: 24 -> 13; matrix products, arithmetic and copies ran while one was open for 10% -> 11% of each run, Pallas kernels for 0% -> 9%
where the time goes in v1:
time: 866 us; the launch traced here: 856 us
  waiting for transfers between devices  470 us (54%)
  blocking collectives  147 us (17%)
  Pallas kernels  73.2 us (8%)
  local copies, waits for them, and re-layouts  65 us (8%)
  matrix products  42.2 us (5%)
  other arithmetic  25.6 us (3%)
  starting transfers between devices  17.3 us (2%)
  between operations  15.7 us (2%)
    reduce_scatter x4, waiting for transfers between devices, scatter(): lax.psum_scatter(grad.astype(jnp.bfloat16), 'seq', scatter_dimension=0, t...  219 us
    all_gather x4, waiting for transfers between devices, gather(): lax.all_gather(jnp.concatenate(parts, axis=1), 'seq', axis=0, tiled=True)  176 us
    psum x1, blocking collectives, shards(): lax.psum((alog_part, dt_part, conv_part, first_norm_piece, second_norm_pi...  74 us
    all_to_all x3, blocking collectives, exchange(): return lax.all_to_all(parts, 'seq', 0, 0)  73 us
    pallas_call x4, Pallas kernels, over_blocks(): pl.pallas_call(kernel, grid=(blocks,), in_specs=[spec(a.shape, i >= cut)...  67.1 us
    all_to_all x2, waiting for transfers between devices, exchange(): return lax.all_to_all(parts, 'seq', 0, 0)  44.7 us
    unnamed x188, local copies, waits for them, and re-layouts  34.5 us
    unnamed x10, waiting for transfers between devices  21 us
  transfers between devices with their start and end apart: 18, of which 13 were waited for; matrix products, arithmetic and copies ran while one was open for 11% of the time, Pallas kernels for 9%

profile of v1, /device:TPU:0, one launch (start us, length us, event | category | flops | bytes accessed | tf_op | source)
XLA Modules:
  0.0 855.8 jit_solution(10741594032266740296)
XLA Ops:
  13.8 96.2 %all-gather.5.cloned.1.call-done = bf16[1024,3080]{1,0:T(8,128)(2,1)} async-done(((bf16[64,3080]{1,0:T(8,128)(2,1)}), bf16[1024,3080]{1,0:T(8,128)(2,1)}) %all-gather.5.cloned.1.call-update) | async-done | bytes 6307856 | tf_op jit(solution)/shard_map/all_gather | solution.py:391
  110.0 4.4 fusion.69
  114.5 3.4 collective-permute-start
  124.7 25.4 %shard_map.347 = (f32[3,4,64,256]{3,2,1,0:T(8,128)S(1)}, f32[3,4,64,128]{3,2,1,0:T(8,128)S(1)}, f32[3,4,128,128]{3,2,1,0:T(8,128)S(1)}, f32[3,4,128,256]{3,2,1,0...) custom-call(f32[3,4,64,128]{3,2,1,0:T(8,128)S(1)} %bitcast.221, f32[3,4,64,128]{3,2,1,0:T(8,128)S(1)} %bitcast.219, ...), custom_call_target="tpu_custom_call" | custom-call | tf_op jit(solution)/shard_map/pallas_call | solution.py:302
  153.2 27.6 %all_to_all.25 = f32[16,128,64]{1,2,0:T(8,128)} all-to-all(f32[16,128,64]{1,2,0:T(8,128)S(1)} %copy.264), channel_id=1, replica_groups=mesh['seq'=16,'head'=2] {'seq'}, dimensions={0} | all-to-all | bytes 1048576 | tf_op jit(solution)/shard_map/all_to_all | solution.py:334
  181.9 4.6 all-to-all-start
  189.5 28.5 %all-to-all-done.matrices = f32[16,128,128]{2,1,0:T(8,128)S(1)} async-done(((f32[16,128,128]{2,1,0:T(8,128)}), f32[16,128,128]{2,1,0:T(8,128)S(1)}, u32[]{:S(2)}, u32[]{:S(2)}) %all-to-all-start) | async-done | bytes 1048608 | tf_op jit(solution)/shard_map/all_to_all | solution.py:334
  219.5 2.7 shard_map.348
  225.6 6.0 all-to-all-start.2
  233.9 16.2 %all-to-all-done.2 = f32[16,128,64]{1,2,0:T(8,128)} async-done(((f32[16,128,64]{1,2,0:T(8,128)}), f32[16,128,64]{1,2,0:T(8,128)}, u32[]{:S(2)}, u32[]{:S(2)}) %all-to-all-start.2) | async-done | bytes 524320 | tf_op jit(solution)/shard_map/all_to_all | solution.py:334
  255.3 3.1 shard_map.349
  264.0 2.6 fusion.70
  270.1 17.9 %all-gather.9.cloned.1.call-done = bf16[1024,2816]{1,0:T(8,128)(2,1)} async-done(((bf16[64,2816]{1,0:T(8,128)(2,1)}), bf16[1024,2816]{1,0:T(8,128)(2,1)}) %all-gather.9.cloned.1.call-update) | async-done | bytes 5767184 | tf_op jit(solution)/shard_map/all_gather | solution.py:391
  287.9 5.6 fusion.53
  293.5 61.7 %all-gather.11.cloned.1.call-done = bf16[1024,1408]{1,0:T(8,128)(2,1)} async-done(((bf16[64,1408]{1,0:T(8,128)(2,1)}), bf16[1024,1408]{1,0:T(8,128)(2,1)}) %all-gather.11.cloned.1.call-update) | async-done | bytes 2883600 | tf_op jit(solution)/shard_map/all_gather | solution.py:391
  355.2 3.7 multiply_convert_fusion.1
  372.3 3.3 convolution_convert_fusion.3
  375.7 3.7 fusion
  379.4 4.6 copy.305
  384.1 2.4 multiply_reduce_fusion.5
  392.7 23.5 %all_to_all.26 = f32[16,128,64]{1,2,0:T(8,128)} all-to-all(f32[16,128,64]{1,2,0:T(8,128)S(1)} %copy.275), channel_id=1, replica_groups=mesh['seq'=16,'head'=2] {'seq'}, dimensions={0} | all-to-all | bytes 1048576 | tf_op jit(solution)/shard_map/all_to_all | solution.py:334
  419.8 3.4 shard_map.351
  425.8 21.9 %all_to_all.27 = f32[16,128,64]{1,2,0:T(8,128)} all-to-all(f32[16,128,64]{1,2,0:T(8,128)S(1)} %copy.277), channel_id=1, replica_groups=mesh['seq'=16,'head'=2] {'seq'}, dimensions={0} | all-to-all | bytes 1048576 | tf_op jit(solution)/shard_map/all_to_all | solution.py:334
  449.0 36.7 %shard_map.352 = (f32[3,4,64,128]{3,2,1,0:T(8,128)S(1)}, f32[3,4,64,128]{3,2,1,0:T(8,128)S(1)}, f32[3,4,64,256]{3,2,1,0:T(8,128)S(1)}, f32[3,4,64,1]{3,2,1,0:T(8...) custom-call(f32[3,4,64,128]{3,2,1,0:T(8,128)S(1)} %bitcast.222, f32[3,4,64,128]{3,2,1,0:T(8,128)S(1)} %bitcast.220, ...), custom_call_target="tpu_custom_call" | custom-call | tf_op jit(solution)/shard_map/pallas_call | solution.py:302
  495.8 3.5 collective-permute-done.4
  502.0 3.6 convolution_convert_fusion.1
  507.1 4.2 convolution_convert_fusion
  512.7 5.2 fusion.72
  520.7 74.0 %all-reduce = (f32[1024]{0:T(1024)}, f32[4,2048]{1,0:T(4,128)S(1)}, f32[4]{0:T(128)}, f32[4]{0:T(128)}, f32[256]{0:T(256)}, /*index=5*/f32[1024]{0:T(1024)}) all-reduce(f32[1024]{0:T(1024)S(1)} %get-tuple-element.174, f32[4,2048]{1,0:T(4,128)S(1)} %pad_maximum_fusion.8, ...), channel_id=1, replica_groups=mesh['seq'=16,'head'=2] {'seq'}, use_global_device_ids=true, to_apply=%region_11.12 | all-reduce | flops 10504 | bytes 84032 | tf_op jit(solution)/shard_map/psum | solution.py:553
  600.3 19.7 %reduce-scatter.16.cloned.1.call-done = bf16[64,1408]{1,0:T(8,128)(2,1)} async-done(((bf16[1024,1408]{1,0:T(8,128)(2,1)}), bf16[64,1408]{1,0:T(8,128)(2,1)}) %reduce-scatter.16.cloned.1.call-update) | async-done | bytes 180240
  622.2 97.1 %reduce-scatter.8.cloned.1.call-done = bf16[64,2056]{1,0:T(8,128)(2,1)} async-done(((bf16[1024,2056]{1,0:T(8,128)(2,1)}), bf16[64,2056]{1,0:T(8,128)(2,1)}) %reduce-scatter.8.cloned.1.call-update) | async-done | bytes 263184 | tf_op jit(solution)/shard_map/reduce_scatter | solution.py:493
  724.7 122.2 %reduce-scatter.14.cloned.1.call-done = bf16[64,2816]{1,0:T(8,128)(2,1)} async-done(((bf16[1024,2816]{1,0:T(8,128)(2,1)}), bf16[64,2816]{1,0:T(8,128)(2,1)}) %reduce-scatter.14.cloned.1.call-update) | async-done | bytes 360464 | tf_op jit(solution)/shard_map/reduce_scatter | solution.py:493
  (333 shorter events, 101.5 us)
Async XLA Ops:
  7.2 102.7 %copy-start.61 = (f32[1024]{0:T(1024)S(1)}, f32[1024]{0:T(1024)}, u32[]{:S(2)}) copy-start(f32[1024]{0:T(1024)} %param.21) | copy-start | bytes 12292
  7.3 102.7 %all-gather.5.cloned.1.call-start = ((), (), s32[]{:S(2)}) async-start(), calls=%async_computation.10 | async-start | bytes 6963200 | tf_op jit(solution)/shard_map/all_gather | solution.py:391
  10.8 253.2 %all-gather.7.cloned.1.call-start = ((), (), s32[]{:S(2)}) async-start(), calls=%async_computation.11 | async-start | bytes 2228224 | tf_op jit(solution)/shard_map/all_gather | solution.py:391
  11.6 276.3 %all-gather.9.cloned.1.call-start = ((), (), s32[]{:S(2)}) async-start(), calls=%async_computation.12 | async-start | bytes 6127616 | tf_op jit(solution)/shard_map/all_gather | solution.py:391
  13.7 104.1 %copy-start.85 = (f32[4]{0:T(128)}, f32[4]{0:T(128)S(1)}, u32[]{:S(2)}) copy-start(f32[4]{0:T(128)S(1)} %exponential_negate_fusion) | copy-start | bytes 52
  13.7 105.8 %copy-start.63 = (f32[1,2048]{1,0:T(1,128)}, f32[1,2048]{1,0:T(1,128)S(1)}, u32[]{:S(2)}) copy-start(f32[1,2048]{1,0:T(1,128)S(1)} %get-tuple-element.219) | copy-start | bytes 24580
  13.7 105.7 %copy-start.65 = (f32[1,2048]{1,0:T(1,128)}, f32[1,2048]{1,0:T(1,128)S(1)}, u32[]{:S(2)}) copy-start(f32[1,2048]{1,0:T(1,128)S(1)} %get-tuple-element.220) | copy-start | bytes 24580
  13.8 105.7 %copy-start.67 = (f32[1,2048]{1,0:T(1,128)}, f32[1,2048]{1,0:T(1,128)S(1)}, u32[]{:S(2)}) copy-start(f32[1,2048]{1,0:T(1,128)S(1)} %get-tuple-element.221) | copy-start | bytes 24580
  13.8 105.7 %copy-start.69 = (f32[1,2048]{1,0:T(1,128)}, f32[1,2048]{1,0:T(1,128)S(1)}, u32[]{:S(2)}) copy-start(f32[1,2048]{1,0:T(1,128)S(1)} %get-tuple-element.222) | copy-start | bytes 24580
  13.8 104.1 %copy-start.83 = (f32[4]{0:T(128)S(1)}, f32[4]{0:T(128)}, u32[]{:S(2)}) copy-start(f32[4]{0:T(128)} %param.32) | copy-start | bytes 52
  114.5 4.8 collective-permute-start
  123.3 26.8 %copy-start.6 = (f32[4,3,64,128]{3,2,0,1:T(8,128)}, f32[4,3,64,128]{3,2,0,1:T(8,128)S(1)}, u32[]{:S(2)}) copy-start(f32[4,3,64,128]{3,2,0,1:T(8,128)S(1)} %copy.353) | copy-start | bytes 1179652
  124.7 25.6 %copy-start.8 = (f32[4,3,64,128]{3,2,0,1:T(8,128)}, f32[4,3,64,128]{3,2,0,1:T(8,128)S(1)}, u32[]{:S(2)}) copy-start(f32[4,3,64,128]{3,2,0,1:T(8,128)S(1)} %copy.354) | copy-start | bytes 1179652
  150.1 237.0 %copy-start.1 = (f32[3,4,128,128]{3,2,1,0:T(8,128)}, f32[3,4,128,128]{3,2,1,0:T(8,128)S(1)}, u32[]{:S(2)}) copy-start(f32[3,4,128,128]{3,2,1,0:T(8,128)S(1)} %get-tuple-element.36.matrix) | copy-start | bytes 2359300
  181.9 36.1 %all-to-all-start = ((f32[16,128,128]{2,1,0:T(8,128)}), f32[16,128,128]{2,1,0:T(8,128)S(1)}, u32[]{:S(2)}, u32[]{:S(2)}) async-start(f32[16,128,128]{2,1,0:T(8,128)} %bitcast.238), calls=%async_computation | async-start | bytes 2097152 | tf_op jit(solution)/shard_map/all_to_all | solution.py:334
  186.5 168.7 %all-gather.11.cloned.1.call-start = ((), (), s32[]{:S(2)}) async-start(), calls=%async_computation.13 | async-start | bytes 3063808 | tf_op jit(solution)/shard_map/all_gather | solution.py:391
  225.6 24.5 %all-to-all-start.2 = ((f32[16,128,64]{1,2,0:T(8,128)}), f32[16,128,64]{1,2,0:T(8,128)}, u32[]{:S(2)}, u32[]{:S(2)}) async-start(f32[16,128,64]{1,2,0:T(8,128)} %copy.266), calls=%async_computation.2 | async-start | bytes 1048576 | tf_op jit(solution)/shard_map/all_to_all | solution.py:334
  231.6 365.5 %reduce-scatter.10.cloned.1.call-start = ((), (), s32[]{:S(2)}) async-start(), calls=%async_computation.15 | async-start | bytes 2228224 | tf_op jit(solution)/shard_map/reduce_scatter | solution.py:493
  266.6 2.4 collective-permute-start.1
  361.5 2.4 collective-permute-start.3
  362.7 2.5 collective-permute-start.2
  372.3 226.4 %reduce-scatter.12.cloned.1.call-start = ((), (), s32[]{:S(2)}) async-start(), calls=%async_computation.16 | async-start | bytes 2228224 | tf_op jit(solution)/shard_map/reduce_scatter | solution.py:493
  375.7 244.3 %reduce-scatter.16.cloned.1.call-start = ((), (), s32[]{:S(2)}) async-start(), calls=%async_computation.18 | async-start | bytes 3063808
  384.1 335.3 %reduce-scatter.8.cloned.1.call-start = ((), (), s32[]{:S(2)}) async-start(), calls=%async_computation.14 | async-start | bytes 4734976 | tf_op jit(solution)/shard_map/reduce_scatter | solution.py:493
  424.1 24.8 %copy-start.7 = (f32[4,3,64,128]{3,2,0,1:T(8,128)S(1)}, f32[4,3,64,128]{3,2,0,1:T(8,128)}, u32[]{:S(2)}) copy-start(f32[4,3,64,128]{3,2,0,1:T(8,128)} %copy-done.6) | copy-start | bytes 1179652
  424.1 24.8 %copy-start.9 = (f32[4,3,64,128]{3,2,0,1:T(8,128)S(1)}, f32[4,3,64,128]{3,2,0,1:T(8,128)}, u32[]{:S(2)}) copy-start(f32[4,3,64,128]{3,2,0,1:T(8,128)} %copy-done.8) | copy-start | bytes 1179652
  424.1 24.8 %copy-start.13 = (f32[3,4,64,128]{3,2,1,0:T(8,128)S(1)}, f32[3,4,64,128]{3,2,1,0:T(8,128)}, u32[]{:S(2)}) copy-start(f32[3,4,64,128]{3,2,1,0:T(8,128)} %copy-done.10) | copy-start | bytes 1179652
  493.2 6.0 collective-permute-start.4
  505.6 341.2 %reduce-scatter.14.cloned.1.call-start = ((), (), s32[]{:S(2)}) async-start(), calls=%async_computation.17 | async-start | bytes 6127616 | tf_op jit(solution)/shard_map/reduce_scatter | solution.py:493
  517.9 78.0 %copy-start.44 = (f32[192,1024]{1,0:T(8,128)S(1)}, f32[192,1024]{1,0:T(8,128)}, u32[]{:S(2)}) copy-start(f32[192,1024]{1,0:T(8,128)} %copy-done.43) | copy-start | bytes 2359300
  517.9 2.4 collective-permute-start.5
  518.0 2.3 collective-permute-start.6
  (75 other events, 183.2 us)
Sparse Core Ops, SparseCore 0:
  11.3 98.6 all-gather.4
  112.8 67.1 all-gather.6
  183.2 104.6 all-gather.8
  290.5 64.6 all-gather.10
  372.4 82.9 reduce-scatter.9
  457.6 79.3 reduce-scatter.11
  539.2 80.7 reduce-scatter.15
  622.3 96.9 reduce-scatter.7
  721.6 125.2 reduce-scatter.13
